TPU v7x, 512 devices: a whole 4x8x8 slice. The times are simulated.
512 devices in a mesh: atoms: 64 (over x, z, core), width: 8 (over y).
Axes of the slice: x: 4, y: 8, z: 8, core: 2. Of those that a mesh axis runs over, the one named last changes fastest.
Arguments:
- tokens: bfloat16 [8192, 8192], P('atoms', 'width'), may hold values from -6 to 6
- dec_bias: float32 [8192], P('width'), may hold values from -3 to 3
- encoder: bfloat16 [8192, 8192], P('atoms', 'width'), may hold values from -1.5 to 1.5
- enc_bias: float32 [8192], P('atoms'), may hold values from -24 to 24
- decoder: bfloat16 [8192, 8192], P('atoms', 'width'), may hold values from -0.25 to 0.25
- atom_ids: int32 [8192, 16], P('atoms'), may hold values from 0 to 8191, as said below
- block_count: int32 [64], P('atoms'), may hold values from 1 to 2, as said below
Outputs:
- residual: bfloat16 [8192, 8192], P('atoms', 'width')
- encoder_grad: bfloat16 [8192, 8192], P('atoms', 'width')
- decoder_grad: bfloat16 [8192, 8192], P('atoms', 'width')
- bias_grad: float32 [8192], P('atoms')
Inputs may be any that keep to these rules, and one draw needn't show every extreme that they name: atom_ids[t, 2g] and atom_ids[t, 2g + 1] are two different atom slots of one owner o (slot // 128 = o), both below o * 128 + 64 block_count[o]; the 8 owners of one token differ. Of the 128 tokens of one index of atoms, at most 24 use any one owner, and in every draw some owner is used by exactly 24 tokens of every index of atoms. `block_count`: every draw has an owner with 2 live blocks and one with a single live block.
All inputs are finite; a program needn't handle non-finite values.
Results may differ from a plain program's by a relative error of at most 0.018.
Values may be sent and summed in bfloat16 or wider, within the bound.
No kernel may reach another device: no remote copies, remote signals or barrier semaphores. Data moves between devices by JAX's collectives and lax.ppermute only.
A program may use at most 64 MiB of HBM per device.

v0:
```python
import jax
import jax.numpy as jnp
from jax import lax
from jax.sharding import PartitionSpec as P

BLOCK = 64
coherence = 128.0
loss_grad = 1.0 / 32.0
epsilon = 1e-06


def coherence_weights(raw_rows, norm_rows, norm_all, alive_rows, alive_all):
    row_total, extent = raw_rows.shape
    row_ids = jnp.arange(row_total)[:, None]
    col_ids = jnp.arange(extent)[None, :]
    norm_pair = norm_rows[:, None] * norm_all[None, :]
    cosine = raw_rows / norm_pair
    on_diagonal = row_ids == col_ids
    coupled = jnp.where(on_diagonal, 0.0, alive_rows[:, None] * alive_all[None, :] * cosine)
    spread = jnp.sum(coupled * cosine, axis=1)
    diag_term = jnp.where(on_diagonal, (spread / (norm_rows * norm_rows))[:, None], 0.0)
    return (4.0 * coherence * (coupled / norm_pair - diag_term)).astype(jnp.bfloat16)


def picked_pair(table, hit_a, hit_b):
    first_pick = jnp.sum(jnp.where(hit_a, table, 0.0), axis=1)
    second_pick = jnp.sum(jnp.where(hit_b, table, 0.0), axis=1)
    return (first_pick, second_pick)


def per_device(tokens, dec_bias, encoder, enc_bias, decoder, atom_ids, block_count):
    tok_dev, width_shard = tokens.shape
    atom_dev = encoder.shape[0]
    owner_total = lax.axis_size("atoms")
    pair_total = atom_ids.shape[1] // 2
    capacity = 3 * tok_dev * pair_total // (2 * owner_total)
    slot_total = owner_total * capacity
    contract = (((1,), (1,)), ((), ()))
    contract_rows = (((0,), (0,)), ((), ()))
    centered = (tokens.astype(jnp.float32) - dec_bias).astype(jnp.bfloat16)
    pair_ids = atom_ids.reshape(tok_dev * pair_total, 2)
    owner_of = pair_ids[:, 0] // atom_dev
    local_atom = pair_ids % atom_dev
    member = (owner_of[:, None] == jnp.arange(owner_total)[None, :]).astype(jnp.int32)
    before = jnp.cumsum(member, axis=0) - member
    slot_of = owner_of * capacity + jnp.sum(before * member, axis=1)
    source_tok = jnp.arange(tok_dev * pair_total) // pair_total
    outgoing = (
        jnp.zeros((slot_total, width_shard), jnp.bfloat16).at[slot_of].set(centered[source_tok])
    )
    slot_tags = jnp.concatenate([local_atom, source_tok[:, None]], axis=1)
    tag_out = jnp.full((slot_total, 3), -1, jnp.int32).at[slot_of].set(slot_tags)
    incoming = lax.all_to_all(outgoing, "atoms", split_axis=0, concat_axis=0, tiled=True)
    tag_in = lax.all_to_all(tag_out, "atoms", split_axis=0, concat_axis=0, tiled=True)
    columns = jnp.arange(atom_dev)[None, :]
    hit_a = tag_in[:, 0:1] == columns
    hit_b = tag_in[:, 1:2] == columns
    scores = lax.dot_general(incoming, encoder, contract, preferred_element_type=jnp.float32)
    scores = lax.psum(scores.astype(jnp.bfloat16), "width").astype(jnp.float32)
    pre_a, pre_b = picked_pair(scores, hit_a, hit_b)
    bias_a, bias_b = picked_pair(enc_bias[None, :], hit_a, hit_b)
    act_a = (pre_a + bias_a).astype(jnp.bfloat16)
    act_b = (pre_b + bias_b).astype(jnp.bfloat16)
    zero_low = jnp.zeros((), jnp.bfloat16)
    act_table = jnp.where(hit_a, act_a[:, None], zero_low) + jnp.where(
        hit_b, act_b[:, None], zero_low
    )
    decoded = jnp.dot(act_table, decoder, preferred_element_type=jnp.float32).astype(jnp.bfloat16)
    returned = lax.all_to_all(decoded, "atoms", split_axis=0, concat_axis=0, tiled=True)
    own_terms = returned[slot_of].reshape(tok_dev, pair_total, width_shard).astype(jnp.float32)
    residual = (jnp.sum(own_terms, axis=1) + dec_bias - tokens.astype(jnp.float32)).astype(
        jnp.bfloat16
    )
    error_out = (
        jnp.zeros((slot_total, width_shard), jnp.bfloat16).at[slot_of].set(residual[source_tok])
    )
    errors = lax.all_to_all(error_out, "atoms", split_axis=0, concat_axis=0, tiled=True)
    back_scores = lax.dot_general(errors, decoder, contract, preferred_element_type=jnp.float32)
    back_scores = lax.psum(back_scores.astype(jnp.bfloat16), "width").astype(jnp.float32)
    grad_a, grad_b = picked_pair(back_scores, hit_a, hit_b)
    dact_a = grad_a * loss_grad
    dact_b = grad_b * loss_grad
    dact_table = jnp.where(hit_a, dact_a[:, None], 0.0) + jnp.where(hit_b, dact_b[:, None], 0.0)
    bias_grad = jnp.sum(dact_table, axis=0)
    encoder_grad = lax.dot_general(
        dact_table.astype(jnp.bfloat16), incoming, contract_rows, preferred_element_type=jnp.float32
    ).astype(jnp.bfloat16)
    fitted = (
        lax.dot_general(act_table, errors, contract_rows, preferred_element_type=jnp.float32)
        * loss_grad
    )
    raw_gram = lax.dot_general(decoder, decoder, contract, preferred_element_type=jnp.float32)
    alive = (jnp.arange(atom_dev) < block_count[0] * BLOCK).astype(jnp.float32)
    summed = lax.psum(raw_gram, "width")
    norms = jnp.sqrt(jnp.diagonal(summed) + epsilon)
    weights = coherence_weights(summed, norms, norms, alive, alive)
    penalty = jnp.dot(weights, decoder, preferred_element_type=jnp.float32)
    decoder_grad = (fitted + penalty).astype(jnp.bfloat16)
    return (residual, encoder_grad, decoder_grad, bias_grad)


def solution(mesh):
    in_specs = (
        P("atoms", "width"),
        P("width"),
        P("atoms", "width"),
        P("atoms"),
        P("atoms", "width"),
        P("atoms", None),
        P("atoms"),
    )
    out_specs = (P("atoms", "width"), P("atoms", "width"), P("atoms", "width"), P("atoms"))
    return jax.shard_map(
        per_device, mesh=mesh, in_specs=in_specs, out_specs=out_specs, check_vma=False
    )
```

profile of v0, /device:TPU:2, one launch (start us, length us, event | category | flops | bytes accessed | tf_op | source)
XLA Modules:
  0.0 508.2 jit_solution(8681748230388222543)
XLA Ops:
  8.9 18.0 %reduce-window.6 = s32[64,8,128]{2,1,0:T(8,128)S(1)} reduce-window(s32[64,8,128]{2,1,0:T(8,128)S(1)} %fusion.41, s32[]{:T(128)} %constant.61.clone.1), window={size=1x1x128 pad=0_0x0_0x127_0}, to_apply=%region_0.1 | reduce-window | flops 8323072 | bytes 524292 | tf_op jit(solution)/shard_map/reduce-window
  29.8 15.7 %scatter_custom_fusion.1 = bf16[1536,1024]{1,0:T(8,128)(2,1)S(1)} fusion(s32[1024]{0:T(1024)S(1)} %get-tuple-element.13, bf16[128,1024]{1,0:T(8,128)(2,1)} %fusion.16, s32[1024]{0:T(1024)S(1)} %broadcast_clamp_fusion.1, bf16[]{:T(256)} %constant.68.clone.1), kind=kCustom, calls=%fused_computation.13 | custom fusion | bytes 3146240 | tf_op jit(solution)/shard_map/scatter | solution.py:49
  45.5 86.1 %all_to_all.48 = bf16[64,24,1024]{2,1,0:T(8,128)(2,1)S(1)} all-to-all(bf16[64,24,1024]{2,1,0:T(8,128)(2,1)S(1)} %bitcast.47), channel_id=1, replica_groups=mesh['atoms'=64,'width'=8] {'atoms'}, dimensions={0} | all-to-all | bytes 6291456 | tf_op jit(solution)/shard_map/all_to_all | solution.py:53
  131.6 1.7 copy-done.4
  133.3 1.7 convolution_convert_fusion.2
  135.3 3.5 scatter_custom_fusion
  139.3 16.6 %all_to_all.49 = s32[64,24,3]{1,2,0:T(4,128)S(1)} all-to-all(s32[64,24,3]{1,2,0:T(4,128)S(1)} %copy.33), channel_id=1, replica_groups=mesh['atoms'=64,'width'=8] {'atoms'}, dimensions={0} | all-to-all | bytes 36864 | tf_op jit(solution)/shard_map/all_to_all | solution.py:54
  156.0 55.8 %all-reduce.4.cloned.1.call-done = bf16[1536,128]{1,0:T(8,128)(2,1)} async-done(((bf16[1536,128]{1,0:T(8,128)(2,1)}), bf16[1536,128]{1,0:T(8,128)(2,1)}) %all-reduce.4.cloned.1.call-update) | async-done | bytes 393232 | tf_op jit(solution)/shard_map/psum | solution.py:59
  211.8 2.5 fusion.8
  214.4 3.1 convolution_convert_fusion
  217.5 10.9 %all-to-all-start.2 = ((bf16[64,24,1024]{2,1,0:T(8,128)(2,1)}), bf16[64,24,1024]{2,1,0:T(8,128)(2,1)S(1)}, u32[]{:S(2)}, u32[]{:S(2)}) async-start(bf16[64,24,1024]{2,1,0:T(8,128)(2,1)} %bitcast.46), calls=%async_computation.2 | async-start | bytes 6291456 | tf_op jit(solution)/shard_map/all_to_all | solution.py:69
  228.4 71.9 %all-to-all-done.2 = bf16[64,24,1024]{2,1,0:T(8,128)(2,1)S(1)} async-done(((bf16[64,24,1024]{2,1,0:T(8,128)(2,1)}), bf16[64,24,1024]{2,1,0:T(8,128)(2,1)S(1)}, u32[]{:S(2)}, u32[]{:S(2)}) %all-to-all-start.2) | async-done | bytes 3145760 | tf_op jit(solution)/shard_map/all_to_all | solution.py:69
  300.4 5.4 %gather_fusion = bf16[1024,1024]{1,0:T(8,128)(2,1)} fusion(bf16[1536,1024]{1,0:T(8,128)(2,1)S(1)} %bitcast.45, s32[1024]{0:T(1024)S(1)} %broadcast_clamp_fusion), kind=kCustom, calls=%fused_computation.1 | custom fusion | bytes 4198400 | tf_op jit(solution)/shard_map/gather | solution.py:70
  305.7 3.0 convert_reduce_fusion
  309.8 14.8 %scatter_custom_fusion.2 = bf16[1536,1024]{1,0:T(8,128)(2,1)} fusion(s32[1024]{0:T(1024)S(1)} %get-tuple-element.13, bf16[128,1024]{1,0:T(8,128)(2,1)S(1)} %fusion.17, s32[1024]{0:T(1024)S(1)} %broadcast_clamp_fusion.1, bf16[]{:T(256)} %constant.68.clone.1), kind=kCustom, calls=%fused_computation.11 | custom fusion | bytes 3145730 | tf_op jit(solution)/shard_map/scatter | solution.py:75
  324.6 7.4 %all-to-all-start.3 = ((bf16[64,24,1024]{2,1,0:T(8,128)(2,1)}), bf16[64,24,1024]{2,1,0:T(8,128)(2,1)}, u32[]{:S(2)}, u32[]{:S(2)}) async-start(bf16[64,24,1024]{2,1,0:T(8,128)(2,1)} %bitcast.9), calls=%async_computation.3 | async-start | bytes 6291456 | tf_op jit(solution)/shard_map/all_to_all | solution.py:77
  334.0 77.4 %all-reduce.8.cloned.1.call-done = f32[128,128]{1,0:T(8,128)} async-done(((f32[128,128]{1,0:T(8,128)}), f32[128,128]{1,0:T(8,128)}) %all-reduce.8.cloned.1.call-update) | async-done | bytes 65552 | tf_op jit(solution)/shard_map/psum | solution.py:94
  411.4 1.9 gather_fusion.1
  414.4 3.6 convolution_convert_fusion.1
  418.4 5.2 %fusion.7 = bf16[128,1024]{1,0:T(8,128)(2,1)} fusion(f32[128,1024]{1,0:T(8,128)S(1)} %fusion.47, bf16[1536,1024]{1,0:T(8,128)(2,1)} %bitcast.10, s32[1536]{0:T(1024)S(1)} %get-tuple-element.9, s32[1536]{0:T(1024)S(1)} %get-tuple-element.8, bf16[1536]{0:T(1024)(128)(2,1)S(1)} %add_convert_fusion, bf16[1536]{0:T(1024)(128)(2,1)S(1)} %add_convert_fusion.1), kind=kOutput, calls=%fused_computation.21 | convolution fusion | flops 404619264 | bytes 3950592 | tf_op jit(solution)/shard_map/dot_general | solution.py:89
  423.6 71.9 %all-reduce.6.cloned.1.call-done = bf16[1536,128]{1,0:T(8,128)(2,1)} async-done(((bf16[1536,128]{1,0:T(8,128)(2,1)}), bf16[1536,128]{1,0:T(8,128)(2,1)}) %all-reduce.6.cloned.1.call-update) | async-done | bytes 393232 | tf_op jit(solution)/shard_map/psum | solution.py:79
  495.6 2.1 fusion.10
  497.7 1.8 fusion.12
  499.4 2.3 convolution_convert_fusion.3
  (64 shorter events, 9.0 us)
Async XLA Ops:
  7.2 207.2 %copy-start = (bf16[128,1024]{1,0:T(8,128)(2,1)S(1)}, bf16[128,1024]{1,0:T(8,128)(2,1)}, u32[]{:S(2)}) copy-start(bf16[128,1024]{1,0:T(8,128)(2,1)} %param.11) | copy-start | bytes 786436
  7.2 21.8 %copy-start.7 = (bf16[128,1024]{1,0:T(8,128)(2,1)S(1)}, bf16[128,1024]{1,0:T(8,128)(2,1)}, u32[]{:S(2)}) copy-start(bf16[128,1024]{1,0:T(8,128)(2,1)} %param.7) | copy-start | bytes 786436
  7.2 21.8 %copy-start.9 = (f32[1024]{0:T(1024)S(1)}, f32[1024]{0:T(1024)}, u32[]{:S(2)}) copy-start(f32[1024]{0:T(1024)} %param.8) | copy-start | bytes 12292
  7.2 204.6 %all-reduce.4.cloned.1.call-start = ((), (), s32[]{:S(2)}) async-start(), calls=%async_computation.4 | async-start | bytes 786432 | tf_op jit(solution)/shard_map/psum | solution.py:59
  8.5 21.3 %copy-start.1 = (s32[1024,2]{1,0:T(8,128)}, s32[1024,2]{1,0:T(8,128)S(1)}, u32[]{:S(2)}) copy-start(s32[1024,2]{1,0:T(8,128)S(1)} %reshape.129) | copy-start | bytes 24580
  45.5 87.8 %copy-start.11 = (bf16[128,1024]{1,0:T(8,128)(2,1)S(1)}, bf16[128,1024]{1,0:T(8,128)(2,1)}, u32[]{:S(2)}) copy-start(bf16[128,1024]{1,0:T(8,128)(2,1)} %param.9) | copy-start | bytes 786436
  131.6 1.7 copy-start.4
  131.6 3.4 copy-start.2
  133.3 2.0 copy-start.6
  135.0 76.8 %copy-start.10 = (f32[128]{0:T(128)S(1)}, f32[128]{0:T(128)}, u32[]{:S(2)}) copy-start(f32[128]{0:T(128)} %param.10) | copy-start | bytes 1540
  217.5 82.9 %all-to-all-start.2 = ((bf16[64,24,1024]{2,1,0:T(8,128)(2,1)}), bf16[64,24,1024]{2,1,0:T(8,128)(2,1)S(1)}, u32[]{:S(2)}, u32[]{:S(2)}) async-start(bf16[64,24,1024]{2,1,0:T(8,128)(2,1)} %bitcast.46), calls=%async_computation.2 | async-start | bytes 6291456 | tf_op jit(solution)/shard_map/all_to_all | solution.py:69
  309.8 14.8 %copy-start.8 = (bf16[128,1024]{1,0:T(8,128)(2,1)}, bf16[128,1024]{1,0:T(8,128)(2,1)S(1)}, u32[]{:S(2)}) copy-start(bf16[128,1024]{1,0:T(8,128)(2,1)S(1)} %fusion.17) | copy-start | bytes 786436
  324.6 89.8 %all-to-all-start.3 = ((bf16[64,24,1024]{2,1,0:T(8,128)(2,1)}), bf16[64,24,1024]{2,1,0:T(8,128)(2,1)}, u32[]{:S(2)}, u32[]{:S(2)}) async-start(bf16[64,24,1024]{2,1,0:T(8,128)(2,1)} %bitcast.9), calls=%async_computation.3 | async-start | bytes 6291456 | tf_op jit(solution)/shard_map/all_to_all | solution.py:77
  332.1 79.3 %all-reduce.8.cloned.1.call-start = ((), (), s32[]{:S(2)}) async-start(), calls=%async_computation.6 | async-start | bytes 131072 | tf_op jit(solution)/shard_map/psum | solution.py:94
  333.0 162.6 %all-reduce.6.cloned.1.call-start = ((), (), s32[]{:S(2)}) async-start(), calls=%async_computation.5 | async-start | bytes 786432 | tf_op jit(solution)/shard_map/psum | solution.py:79
  413.3 4.8 copy-start.3
  418.1 81.4 %copy-start.5 = (bf16[64,24,1024]{2,1,0:T(8,128)(2,1)S(1)}, bf16[64,24,1024]{2,1,0:T(8,128)(2,1)}, u32[]{:S(2)}) copy-start(bf16[64,24,1024]{2,1,0:T(8,128)(2,1)} %copy-done.4) | copy-start | bytes 9437188
Sparse Core Ops, SparseCore 0:
  135.2 76.6 all-reduce.3
  335.7 75.5 all-reduce.7
  418.2 77.2 all-reduce.5
where the time goes:
time: 509 us; the launch traced here: 508 us
  waiting for transfers between devices  277 us (54%)
  blocking collectives  103 us (20%)
  local copies, waits for them, and re-layouts  41.7 us (8%)
  other arithmetic  36.1 us (7%)
  starting transfers between devices  18.7 us (4%)
  matrix products  17.1 us (3%)
  between operations  14.7 us (3%)
    all_to_all x1, blocking collectives, per_device(): lax.all_to_all(outgoing, 'atoms', split_axis=0, concat_axis=0, tiled=True)  86.1 us
    psum x1, waiting for transfers between devices, per_device(): summed = lax.psum(raw_gram, 'width')  77.4 us
    psum x1, waiting for transfers between devices, per_device(): lax.psum(back_scores.astype(jnp.bfloat16), 'width').astype(jnp.float32)  71.9 us
    all_to_all x1, waiting for transfers between devices, per_device(): lax.all_to_all(decoded, 'atoms', split_axis=0, concat_axis=0, tiled=True)  71.9 us
    psum x1, waiting for transfers between devices, per_device(): scores = lax.psum(scores.astype(jnp.bfloat16), 'width').astype(jnp.float32)  55.8 us
    scatter x2, local copies, waits for them, and re-layouts, per_device(): jnp.zeros((slot_total, width_shard), jnp.bfloat16).at[slot_of]  30.5 us
    another operation x3, other arithmetic  18.2 us
    all_to_all x1, blocking collectives, per_device(): lax.all_to_all(tag_out, 'atoms', split_axis=0, concat_axis=0, tiled=True)  16.6 us
  transfers between devices with their start and end apart: 5, of which 4 were waited for; matrix products, arithmetic and copies ran while one was open for 3% of the time, Pallas kernels for 0%

commit v1 on v0

--- a/solution.py
+++ b/solution.py
@@ -56,7 +56,9 @@
     hit_a = tag_in[:, 0:1] == columns
     hit_b = tag_in[:, 1:2] == columns
     scores = lax.dot_general(incoming, encoder, contract, preferred_element_type=jnp.float32)
-    scores = lax.psum(scores.astype(jnp.bfloat16), "width").astype(jnp.float32)
+    scores = jnp.sum(lax.all_gather(scores.astype(jnp.bfloat16), "width"), axis=0).astype(
+        jnp.float32
+    )
     pre_a, pre_b = picked_pair(scores, hit_a, hit_b)
     bias_a, bias_b = picked_pair(enc_bias[None, :], hit_a, hit_b)
     act_a = (pre_a + bias_a).astype(jnp.bfloat16)

time: 509 us -> 480 us (0.943)
  waiting for transfers between devices: 277 us -> 247 us
    psum x1 -> x0, waiting for transfers between devices: 55.8 us -> none  [per_device(): scores = lax.psum(scores.astype(jnp.bfloat16), 'width').astype(jnp.float32)]
    all_gather x0 -> x1, waiting for transfers between devices: none -> 24.8 us  [per_device(): lax.all_gather(scores.astype(jnp.bfloat16), 'width')]
where the time goes in v1:
time: 480 us; the launch traced here: 479 us
  waiting for transfers between devices  247 us (51%)
  blocking collectives  103 us (21%)
  local copies, waits for them, and re-layouts  41.7 us (9%)
  other arithmetic  37.8 us (8%)
  starting transfers between devices  18.7 us (4%)
  matrix products  17.1 us (4%)
  between operations  14.7 us (3%)
    all_to_all x1, blocking collectives, per_device(): lax.all_to_all(outgoing, 'atoms', split_axis=0, concat_axis=0, tiled=True)  86.1 us
    psum x1, waiting for transfers between devices, per_device(): summed = lax.psum(raw_gram, 'width')  77.7 us
    psum x1, waiting for transfers between devices, per_device(): lax.psum(back_scores.astype(jnp.bfloat16), 'width').astype(jnp.float32)  72 us
    all_to_all x1, waiting for transfers between devices, per_device(): lax.all_to_all(decoded, 'atoms', split_axis=0, concat_axis=0, tiled=True)  71.9 us
    scatter x2, local copies, waits for them, and re-layouts, per_device(): jnp.zeros((slot_total, width_shard), jnp.bfloat16).at[slot_of]  30.5 us
    all_gather x1, waiting for transfers between devices, per_device(): lax.all_gather(scores.astype(jnp.bfloat16), 'width')  24.8 us
    another operation x3, other arithmetic  18.2 us
    all_to_all x1, blocking collectives, per_device(): lax.all_to_all(tag_out, 'atoms', split_axis=0, concat_axis=0, tiled=True)  16.6 us
  transfers between devices with their start and end apart: 5, of which 4 were waited for; matrix products, arithmetic and copies ran while one was open for 3% of the time, Pallas kernels for 0%

profile of v1, /device:TPU:2, one launch (start us, length us, event | category | flops | bytes accessed | tf_op | source)
XLA Modules:
  0.0 479.3 jit_solution(8614170217119970)
XLA Ops:
  8.9 18.0 %reduce-window.6 = s32[64,8,128]{2,1,0:T(8,128)S(1)} reduce-window(s32[64,8,128]{2,1,0:T(8,128)S(1)} %fusion.41, s32[]{:T(128)} %constant.62.clone.1), window={size=1x1x128 pad=0_0x0_0x127_0}, to_apply=%region_0.1 | reduce-window | flops 8323072 | bytes 524292 | tf_op jit(solution)/shard_map/reduce-window
  29.8 15.7 %scatter_custom_fusion.1 = bf16[1536,1024]{1,0:T(8,128)(2,1)S(1)} fusion(s32[1024]{0:T(1024)S(1)} %get-tuple-element.13, bf16[128,1024]{1,0:T(8,128)(2,1)} %fusion.16, s32[1024]{0:T(1024)S(1)} %broadcast_clamp_fusion.1, bf16[]{:T(256)} %constant.69.clone.1), kind=kCustom, calls=%fused_computation.13 | custom fusion | bytes 3146240 | tf_op jit(solution)/shard_map/scatter | solution.py:49
  45.5 86.1 %all_to_all.48 = bf16[64,24,1024]{2,1,0:T(8,128)(2,1)S(1)} all-to-all(bf16[64,24,1024]{2,1,0:T(8,128)(2,1)S(1)} %bitcast.48), channel_id=1, replica_groups=mesh['atoms'=64,'width'=8] {'atoms'}, dimensions={0} | all-to-all | bytes 6291456 | tf_op jit(solution)/shard_map/all_to_all | solution.py:53
  131.6 1.7 copy-done.4
  133.3 1.7 convolution_convert_fusion.2
  135.3 3.5 scatter_custom_fusion
  139.3 16.6 %all_to_all.49 = s32[64,24,3]{1,2,0:T(4,128)S(1)} all-to-all(s32[64,24,3]{1,2,0:T(4,128)S(1)} %copy.33), channel_id=1, replica_groups=mesh['atoms'=64,'width'=8] {'atoms'}, dimensions={0} | all-to-all | bytes 36864 | tf_op jit(solution)/shard_map/all_to_all | solution.py:54
  156.0 24.8 %all-gather.3.cloned.1.call-done = bf16[12288,128]{1,0:T(8,128)(2,1)} async-done(((bf16[1536,128]{1,0:T(8,128)(2,1)}), bf16[12288,128]{1,0:T(8,128)(2,1)}) %all-gather.3.cloned.1.call-update) | async-done | bytes 3145744 | tf_op jit(solution)/shard_map/all_gather | solution.py:59
  180.9 2.5 reduce_sum.106
  185.0 3.1 convolution_convert_fusion
  188.1 10.9 %all-to-all-start.2 = ((bf16[64,24,1024]{2,1,0:T(8,128)(2,1)}), bf16[64,24,1024]{2,1,0:T(8,128)(2,1)S(1)}, u32[]{:S(2)}, u32[]{:S(2)}) async-start(bf16[64,24,1024]{2,1,0:T(8,128)(2,1)} %bitcast.47), calls=%async_computation.2 | async-start | bytes 6291456 | tf_op jit(solution)/shard_map/all_to_all | solution.py:71
  199.1 71.9 %all-to-all-done.2 = bf16[64,24,1024]{2,1,0:T(8,128)(2,1)S(1)} async-done(((bf16[64,24,1024]{2,1,0:T(8,128)(2,1)}), bf16[64,24,1024]{2,1,0:T(8,128)(2,1)S(1)}, u32[]{:S(2)}, u32[]{:S(2)}) %all-to-all-start.2) | async-done | bytes 3145760 | tf_op jit(solution)/shard_map/all_to_all | solution.py:71
  271.0 5.4 %gather_fusion = bf16[1024,1024]{1,0:T(8,128)(2,1)} fusion(bf16[1536,1024]{1,0:T(8,128)(2,1)S(1)} %bitcast.46, s32[1024]{0:T(1024)S(1)} %broadcast_clamp_fusion), kind=kCustom, calls=%fused_computation.1 | custom fusion | bytes 4198400 | tf_op jit(solution)/shard_map/gather | solution.py:72
  276.4 3.0 convert_reduce_fusion
  280.4 14.8 %scatter_custom_fusion.2 = bf16[1536,1024]{1,0:T(8,128)(2,1)} fusion(s32[1024]{0:T(1024)S(1)} %get-tuple-element.13, bf16[128,1024]{1,0:T(8,128)(2,1)S(1)} %fusion.17, s32[1024]{0:T(1024)S(1)} %broadcast_clamp_fusion.1, bf16[]{:T(256)} %constant.69.clone.1), kind=kCustom, calls=%fused_computation.11 | custom fusion | bytes 3145730 | tf_op jit(solution)/shard_map/scatter | solution.py:77
  295.3 7.4 %all-to-all-start.3 = ((bf16[64,24,1024]{2,1,0:T(8,128)(2,1)}), bf16[64,24,1024]{2,1,0:T(8,128)(2,1)}, u32[]{:S(2)}, u32[]{:S(2)}) async-start(bf16[64,24,1024]{2,1,0:T(8,128)(2,1)} %bitcast.10), calls=%async_computation.3 | async-start | bytes 6291456 | tf_op jit(solution)/shard_map/all_to_all | solution.py:79
  304.6 77.7 %all-reduce.5.cloned.1.call-done = f32[128,128]{1,0:T(8,128)} async-done(((f32[128,128]{1,0:T(8,128)}), f32[128,128]{1,0:T(8,128)}) %all-reduce.5.cloned.1.call-update) | async-done | bytes 65552 | tf_op jit(solution)/shard_map/psum | solution.py:96
  382.3 1.9 gather_fusion.1
  385.4 3.6 convolution_convert_fusion.1
  389.3 5.2 %fusion.7 = bf16[128,1024]{1,0:T(8,128)(2,1)} fusion(f32[128,1024]{1,0:T(8,128)S(1)} %fusion.47, bf16[1536,1024]{1,0:T(8,128)(2,1)} %bitcast.11, s32[1536]{0:T(1024)S(1)} %get-tuple-element.9, s32[1536]{0:T(1024)S(1)} %get-tuple-element.8, bf16[1536]{0:T(1024)(128)(2,1)S(1)} %add_convert_fusion, bf16[1536]{0:T(1024)(128)(2,1)S(1)} %add_convert_fusion.1), kind=kOutput, calls=%fused_computation.21 | convolution fusion | flops 404619264 | bytes 3950592 | tf_op jit(solution)/shard_map/dot_general | solution.py:91
  394.5 72.0 %all-reduce.3.cloned.1.call-done = bf16[1536,128]{1,0:T(8,128)(2,1)} async-done(((bf16[1536,128]{1,0:T(8,128)(2,1)}), bf16[1536,128]{1,0:T(8,128)(2,1)}) %all-reduce.3.cloned.1.call-update) | async-done | bytes 393232 | tf_op jit(solution)/shard_map/psum | solution.py:81
  466.6 2.1 fusion.10
  468.7 1.8 fusion.12
  470.4 2.3 convolution_convert_fusion.3
  (65 shorter events, 10.6 us)
Async XLA Ops:
  7.2 177.9 %copy-start = (bf16[128,1024]{1,0:T(8,128)(2,1)S(1)}, bf16[128,1024]{1,0:T(8,128)(2,1)}, u32[]{:S(2)}) copy-start(bf16[128,1024]{1,0:T(8,128)(2,1)} %param.11) | copy-start | bytes 786436
  7.2 21.8 %copy-start.7 = (bf16[128,1024]{1,0:T(8,128)(2,1)S(1)}, bf16[128,1024]{1,0:T(8,128)(2,1)}, u32[]{:S(2)}) copy-start(bf16[128,1024]{1,0:T(8,128)(2,1)} %param.7) | copy-start | bytes 786436
  7.2 21.8 %copy-start.9 = (f32[1024]{0:T(1024)S(1)}, f32[1024]{0:T(1024)}, u32[]{:S(2)}) copy-start(f32[1024]{0:T(1024)} %param.8) | copy-start | bytes 12292
  7.2 173.7 %all-gather.3.cloned.1.call-start = ((), (), s32[]{:S(2)}) async-start(), calls=%async_computation.6 | async-start | bytes 3538944 | tf_op jit(solution)/shard_map/all_gather | solution.py:59
  8.5 21.3 %copy-start.1 = (s32[1024,2]{1,0:T(8,128)}, s32[1024,2]{1,0:T(8,128)S(1)}, u32[]{:S(2)}) copy-start(s32[1024,2]{1,0:T(8,128)S(1)} %reshape.129) | copy-start | bytes 24580
  45.5 87.8 %copy-start.11 = (bf16[128,1024]{1,0:T(8,128)(2,1)S(1)}, bf16[128,1024]{1,0:T(8,128)(2,1)}, u32[]{:S(2)}) copy-start(bf16[128,1024]{1,0:T(8,128)(2,1)} %param.9) | copy-start | bytes 786436
  131.6 1.7 copy-start.4
  131.6 3.4 copy-start.2
  133.3 2.0 copy-start.6
  135.3 48.1 %copy-start.10 = (f32[128]{0:T(128)S(1)}, f32[128]{0:T(128)}, u32[]{:S(2)}) copy-start(f32[128]{0:T(128)} %param.10) | copy-start | bytes 1540
  188.1 82.9 %all-to-all-start.2 = ((bf16[64,24,1024]{2,1,0:T(8,128)(2,1)}), bf16[64,24,1024]{2,1,0:T(8,128)(2,1)S(1)}, u32[]{:S(2)}, u32[]{:S(2)}) async-start(bf16[64,24,1024]{2,1,0:T(8,128)(2,1)} %bitcast.47), calls=%async_computation.2 | async-start | bytes 6291456 | tf_op jit(solution)/shard_map/all_to_all | solution.py:71
  280.4 14.8 %copy-start.8 = (bf16[128,1024]{1,0:T(8,128)(2,1)}, bf16[128,1024]{1,0:T(8,128)(2,1)S(1)}, u32[]{:S(2)}) copy-start(bf16[128,1024]{1,0:T(8,128)(2,1)S(1)} %fusion.17) | copy-start | bytes 786436
  295.3 90.1 %all-to-all-start.3 = ((bf16[64,24,1024]{2,1,0:T(8,128)(2,1)}), bf16[64,24,1024]{2,1,0:T(8,128)(2,1)}, u32[]{:S(2)}, u32[]{:S(2)}) async-start(bf16[64,24,1024]{2,1,0:T(8,128)(2,1)} %bitcast.10), calls=%async_computation.3 | async-start | bytes 6291456 | tf_op jit(solution)/shard_map/all_to_all | solution.py:79
  302.7 79.6 %all-reduce.5.cloned.1.call-start = ((), (), s32[]{:S(2)}) async-start(), calls=%async_computation.5 | async-start | bytes 131072 | tf_op jit(solution)/shard_map/psum | solution.py:96
  303.6 162.9 %all-reduce.3.cloned.1.call-start = ((), (), s32[]{:S(2)}) async-start(), calls=%async_computation.4 | async-start | bytes 786432 | tf_op jit(solution)/shard_map/psum | solution.py:81
  384.2 4.8 copy-start.3
  389.0 81.4 %copy-start.5 = (bf16[64,24,1024]{2,1,0:T(8,128)(2,1)S(1)}, bf16[64,24,1024]{2,1,0:T(8,128)(2,1)}, u32[]{:S(2)}) copy-start(bf16[64,24,1024]{2,1,0:T(8,128)(2,1)} %copy-done.4) | copy-start | bytes 9437188
Sparse Core Ops, SparseCore 0:
  135.2 45.6 all-gather.2
  306.4 75.8 all-reduce.4
  389.2 77.3 all-reduce.2
